TPU v7x, 32 devices: a whole 2x2x4 slice. The times are simulated.
32 devices in a mesh: replica: 8 (over y, x, core), tensor: 4 (over z).
Axes of the slice: x: 2, y: 2, z: 4, core: 2. Of those that a mesh axis runs over, the one named last changes fastest.
Arguments:
- queries: bfloat16 [8, 512, 2560], P('replica', None, 'tensor'), may hold values from -160 to 160
- key_rows: bfloat16 [8, 512, 2560], P('replica', None, 'tensor'), may hold values from -4 to 4
- value_rows: bfloat16 [8, 512, 2560], P('replica', None, 'tensor'), may hold values from -6 to 6
- out_grads: bfloat16 [8, 512, 1024], P('replica', 'tensor'), may hold values from -6 to 6
- inner_weights: bfloat16 [8, 20, 128, 1024], P('replica', 'tensor'), may hold values from -0.15625 to 0.15625
- adam_first: bfloat16 [8, 20, 128, 1024], P('replica', 'tensor'), may hold values from -12 to 12
- adam_second: bfloat16 [8, 20, 128, 1024], P('replica', 'tensor'), may hold values from 1 to 16
- anchor: bfloat16 [20, 128, 1024], P('tensor'), may hold values from -0.125 to 0.125
- momentum: float32 [20, 128, 1024], P('tensor', 'replica'), may hold values from -0.06 to 0.06
Outputs:
- query_grads: bfloat16 [8, 512, 2560], P('replica', None, 'tensor')
- key_grads: bfloat16 [8, 512, 2560], P('replica', None, 'tensor')
- value_grads: bfloat16 [8, 512, 2560], P('replica', None, 'tensor')
- new_first: bfloat16 [8, 20, 128, 1024], P('replica', 'tensor')
- new_second: bfloat16 [8, 20, 128, 1024], P('replica', 'tensor')
- new_anchor: bfloat16 [20, 128, 1024], P('tensor')
- new_momentum: float32 [20, 128, 1024], P('tensor', 'replica')
All inputs are finite; a program needn't handle non-finite values.
Results may differ from a plain program's by a relative error of at most 0.028.
Values may be sent and summed in bfloat16 or wider, within the bound.
A program may use at most 64 MiB of HBM per device.

v0:
```python
import math

import jax
import jax.numpy as jnp
from jax import lax
from jax.sharding import PartitionSpec as P

DH = 128


beta_first = 0.9
beta_second = 0.95
correct_first = 0.9999734386011124
correct_second = 0.994079470779666
inner_rate = 0.01
decay_rate = 0.1
epsilon = 1e-08
outer_rate = 0.7
outer_beta = 0.9


def local(
    queries,
    key_rows,
    value_rows,
    out_grads,
    inner_weights,
    adam_first,
    adam_second,
    anchor,
    momentum,
):
    length = queries.shape[1]
    inner_width = queries.shape[2]
    head_count = inner_width // DH
    model_width = out_grads.shape[2]
    score_scale = 1.0 / math.sqrt(DH)
    query_heads = queries[0].reshape(length, head_count, DH)
    key_heads = key_rows[0].reshape(length, head_count, DH)
    value_heads = value_rows[0].reshape(length, head_count, DH)
    scores = (
        jnp.einsum("qhc,khc->hqk", query_heads, key_heads, preferred_element_type=jnp.float32)
        * score_scale
    )
    probs = jax.nn.softmax(scores, axis=-1)
    probs_low = probs.astype(jnp.bfloat16)
    attention = jnp.einsum(
        "hqk,khc->qhc", probs_low, value_heads, preferred_element_type=jnp.float32
    ).astype(jnp.bfloat16)
    attention_rows = attention.reshape(length, inner_width)
    proj_rows = inner_weights[0].reshape(inner_width, model_width)
    block_rows = lax.all_gather(out_grads[0], "tensor", axis=0, tiled=True)
    product_rows = lax.dot_general(
        block_rows, proj_rows, (((1,), (1,)), ((), ())), preferred_element_type=jnp.float32
    ).astype(jnp.bfloat16)
    grad_rows = product_rows
    gradient = lax.dot_general(
        attention_rows, block_rows, (((0,), (0,)), ((), ())), preferred_element_type=jnp.float32
    )
    grad_rows, gradient = (grad_rows, gradient)
    grad_attn = grad_rows.reshape(length, head_count, DH)
    value_grads = jnp.einsum(
        "hqk,qhc->khc", probs_low, grad_attn, preferred_element_type=jnp.float32
    ).astype(jnp.bfloat16)
    grad_probs = jnp.einsum(
        "qhc,khc->hqk", grad_attn, value_heads, preferred_element_type=jnp.float32
    )
    row_dot = jnp.einsum("qhc,qhc->hq", grad_attn, attention, preferred_element_type=jnp.float32)
    grad_scores = (probs * (grad_probs - row_dot[:, :, None])).astype(jnp.bfloat16)
    query_grads = (
        jnp.einsum("hqk,khc->qhc", grad_scores, key_heads, preferred_element_type=jnp.float32)
        * score_scale
    ).astype(jnp.bfloat16)
    key_grads = (
        jnp.einsum("hqk,qhc->khc", grad_scores, query_heads, preferred_element_type=jnp.float32)
        * score_scale
    ).astype(jnp.bfloat16)
    grad_proj = gradient.reshape(head_count, DH, model_width)
    first_moment = beta_first * adam_first[0].astype(jnp.float32) + (1.0 - beta_first) * grad_proj
    second_moment = (
        beta_second * adam_second[0].astype(jnp.float32)
        + (1.0 - beta_second) * grad_proj * grad_proj
    )
    previous = inner_weights[0].astype(jnp.float32)
    stepped = previous - inner_rate * (
        first_moment / correct_first / (jnp.sqrt(second_moment / correct_second) + epsilon)
        + decay_rate * previous
    )
    anchor_wide = anchor.astype(jnp.float32)
    delta_terms = (anchor_wide - stepped).astype(jnp.bfloat16).astype(jnp.float32)
    workers = lax.axis_size("replica")
    slab = momentum.shape[1]
    portion = lax.psum_scatter(
        delta_terms.astype(jnp.bfloat16), "replica", scatter_dimension=1, tiled=True
    ).astype(jnp.float32)
    average = portion / workers
    new_momentum = outer_beta * momentum + average
    anchor_part = lax.dynamic_slice_in_dim(anchor_wide, lax.axis_index("replica") * slab, slab, 1)
    updated = (anchor_part - outer_rate * (average + outer_beta * new_momentum)).astype(
        jnp.bfloat16
    )
    new_anchor = lax.all_gather(updated, "replica", axis=1, tiled=True)
    return (
        query_grads.reshape(length, inner_width)[None],
        key_grads.reshape(length, inner_width)[None],
        value_grads.reshape(length, inner_width)[None],
        first_moment.astype(jnp.bfloat16)[None],
        second_moment.astype(jnp.bfloat16)[None],
        new_anchor,
        new_momentum,
    )


def solution(mesh):
    in_specs = (
        P("replica", None, "tensor"),
        P("replica", None, "tensor"),
        P("replica", None, "tensor"),
        P("replica", "tensor", None),
        P("replica", "tensor", None, None),
        P("replica", "tensor", None, None),
        P("replica", "tensor", None, None),
        P("tensor", None, None),
        P("tensor", "replica", None),
    )
    out_specs = (
        P("replica", None, "tensor"),
        P("replica", None, "tensor"),
        P("replica", None, "tensor"),
        P("replica", "tensor", None, None),
        P("replica", "tensor", None, None),
        P("tensor", None, None),
        P("tensor", "replica", None),
    )
    return jax.shard_map(local, mesh=mesh, in_specs=in_specs, out_specs=out_specs, check_vma=False)
```

profile of v0, /device:TPU:0, one launch (start us, length us, event | category | flops | bytes accessed | tf_op | source)
XLA Modules:
  0.0 125.8 jit_solution(16689872000383346448)
XLA Ops:
  7.2 0.0 all-gather.6.cloned.1.call-start
  7.2 0.7 all-gather.6.cloned.1.call-update
  7.9 0.0 reduce-scatter.2.cloned.1.call-start
  8.0 1.3 %copy.32 = bf16[1,512,640]{1,2,0:T(8,128)(2,1)S(1)} copy(bf16[1,512,640]{2,1,0:T(8,128)(2,1)} %param.9) | data formatting | bytes 1310720 | tf_op args[0]
  9.3 1.6 %copy.33 = bf16[1,512,640]{1,2,0:T(8,128)(2,1)S(1)} copy(bf16[1,512,640]{2,1,0:T(8,128)(2,1)} %param.10) | data formatting | bytes 1310720 | tf_op args[1]
  10.9 1.1 copy.37
  12.0 4.1 %fusion.25 = (f32[5,512]{1,0:T(8,128)S(1)}, f32[5,512,512]{1,2,0:T(8,128)}) fusion(bf16[512,5,128]{0,2,1:T(8,128)(2,1)S(1)} %bitcast.86, bf16[512,5,128]{0,2,1:T(8,128)(2,1)S(1)} %bitcast.82), kind=kOutput, calls=%fused_computation.39 | convolution fusion | flops 339476992 | bytes 6563840 | tf_op jit(solution)/shard_map/sub | solution.py:45
  16.1 3.2 %fusion.10 = bf16[5,512,512]{1,2,0:T(8,128)(2,1)S(1)} fusion(f32[5,512,512]{1,2,0:T(8,128)} %get-tuple-element.27, f32[5,512]{1,0:T(8,128)S(1)} %get-tuple-element.26), kind=kLoop, calls=%fused_computation.16 | loop fusion | flops 2621440 | bytes 7874560 | tf_op jit(solution)/shard_map/convert_element_type | solution.py:46
  19.3 20.9 %all-gather.6.cloned.1.call-done = bf16[1,512,1024]{2,1,0:T(8,128)(2,1)} async-done(((bf16[1,128,1024]{2,1,0:T(8,128)(2,1)}), bf16[1,512,1024]{2,1,0:T(8,128)(2,1)}) %all-gather.6.cloned.1.call-update) | async-done | bytes 1048592 | tf_op jit(solution)/shard_map/all_gather | solution.py:52
  40.3 3.5 %convolution_convert_fusion = bf16[512,640]{1,0:T(8,128)(2,1)} fusion(bf16[640,1024]{1,0:T(8,128)(2,1)} %bitcast.89, bf16[1,512,1024]{2,1,0:T(8,128)(2,1)} %all-gather.6.cloned.1.call-done), kind=kOutput, calls=%fused_computation.22 | convolution fusion | flops 671416320 | bytes 3014656 | tf_op jit(solution)/shard_map/dot_general | solution.py:53
  43.8 1.3 %copy.36 = bf16[512,640]{0,1:T(8,128)(2,1)S(1)} copy(bf16[512,640]{1,0:T(8,128)(2,1)} %convolution_convert_fusion) | data formatting | bytes 1310720 | tf_op jit(solution)/shard_map/convert_element_type | solution.py:55
  45.1 0.0 copy-start.2
  45.2 1.8 %fusion.17 = (f32[5,512]{1,0:T(8,128)S(1)}, bf16[5,512,128]{1,2,0:T(8,128)(2,1)S(1)}) fusion(bf16[5,512,128]{1,2,0:T(8,128)(2,1)S(1)} %bitcast.77, bf16[512,5,128]{0,2,1:T(8,128)(2,1)} %bitcast.80, bf16[5,512,512]{1,2,0:T(8,128)(2,1)S(1)} %fusion.10), kind=kOutput, calls=%fused_computation.29 | convolution fusion | flops 337180160 | bytes 4597760 | tf_op jit(solution)/shard_map/hqk,khc->qhc/dot_general | solution.py:47
  46.9 0.1 copy-done.6
  47.0 0.4 copy-done.7
  47.4 5.9 %fusion.7 = (bf16[5,128,1024]{2,1,0:T(8,128)(2,1)}, bf16[1,5,128,1024]{3,2,1,0:T(8,128)(2,1)}, bf16[1,5,128,1024]{3,2,1,0:T(8,128)(2,1)}) fusion(bf16[1,5,128,1024]{3,2,1,0:T(8,128)(2,1)S(1)} %copy-done.7, bf16[1,5,128,1024]{3,2,1,0:T(8,128)(2,1)} %param.15, bf16[1,5,128,1024]{3,2,1,0:T(8,128)(2,1)S(1)} %copy-done.6, ...), kind=kOutput, calls=%fused_computation.11 | convolution fusion | flops 686161920 | bytes 10878976 | tf_op jit(solution)/shard_map/dot_general | solution.py:57
  53.3 0.0 reduce-scatter.2.cloned.1.call-update
  53.3 0.0 all-gather.4.cloned.1.call-start
  53.4 3.1 %convert_element_type.82 = f32[5,128,1024]{2,1,0:T(8,128)} convert(bf16[5,128,1024]{2,1,0:T(8,128)(2,1)} %param.16) | non-fusion elementwise | flops 655360 | bytes 3932160 | tf_op jit(solution)/shard_map/convert_element_type | solution.py:89
  56.5 33.6 %reduce-scatter.2.cloned.1.call-done = bf16[5,16,1024]{2,1,0:T(8,128)(2,1)} async-done(((bf16[5,128,1024]{2,1,0:T(8,128)(2,1)}), bf16[5,16,1024]{2,1,0:T(8,128)(2,1)}) %reduce-scatter.2.cloned.1.call-update) | async-done | bytes 163856 | tf_op jit(solution)/shard_map/reduce_scatter | solution.py:93
  90.1 2.0 %subtract_convert_fusion = (bf16[5,16,1024]{2,1,0:T(8,128)(2,1)}, f32[5,16,1024]{2,1,0:T(8,128)}) fusion(bf16[5,16,1024]{2,1,0:T(8,128)(2,1)} %reduce-scatter.2.cloned.1.call-done, f32[5,128,1024]{2,1,0:T(8,128)} %convert_element_type.82, s32[]{:T(128)S(6)} %select_n.3, f32[5,16,1024]{2,1,0:T(8,128)} %param.17), kind=kLoop, calls=%fused_computation.35 | loop fusion | flops 737280 | bytes 1310724 | tf_op jit(solution)/shard_map/convert_element_type | solution.py:99
  92.1 0.0 all-gather.4.cloned.1.call-update
  92.1 3.7 %multiply_convert_fusion = bf16[5,512,512]{1,2,0:T(8,128)(2,1)S(1)} fusion(f32[5,512]{1,0:T(8,128)S(1)} %get-tuple-element.28, bf16[512,5,128]{0,2,1:T(8,128)(2,1)S(1)} %bitcast.78, bf16[512,5,128]{0,2,1:T(8,128)(2,1)} %bitcast.81, f32[5,512,512]{1,2,0:T(8,128)} %get-tuple-element.27, f32[5,512]{1,0:T(8,128)S(1)} %get-tuple-element.26), kind=kOutput, calls=%fused_computation.1 | convolution fusion | flops 340787200 | bytes 9195520 | tf_op jit(solution)/shard_map/qhc,khc->hqk/dot_general | solution.py:65
  95.8 1.5 %copy-done = bf16[5,512,512]{1,2,0:T(8,128)(2,1)} copy-done((bf16[5,512,512]{1,2,0:T(8,128)(2,1)}, bf16[5,512,512]{1,2,0:T(8,128)(2,1)S(1)}, u32[]{:S(2)}) %copy-start) | copy-done | bytes 2621464
  97.3 1.8 %fusion.12 = bf16[5,512,128]{1,2,0:T(8,128)(2,1)} fusion(bf16[5,512,512]{1,2,0:T(8,128)(2,1)S(1)} %multiply_convert_fusion, bf16[512,5,128]{0,2,1:T(8,128)(2,1)S(1)} %bitcast.87), kind=kOutput, calls=%fused_computation.20 | convolution fusion | flops 336199680 | bytes 3932160 | tf_op jit(solution)/shard_map/hqk,qhc->khc/dot_general | solution.py:75
  99.1 2.2 %copy.46 = bf16[1,512,640]{2,1,0:T(8,128)(2,1)} copy(bf16[1,512,640]{1,2,0:T(8,128)(2,1)} %bitcast.88) | data formatting | bytes 1310720
  101.3 3.3 %fusion.13 = bf16[5,512,128]{1,2,0:T(8,128)(2,1)} fusion(bf16[512,5,128]{0,2,1:T(8,128)(2,1)} %bitcast.83, bf16[5,512,512]{1,2,0:T(8,128)(2,1)} %copy-done), kind=kOutput, calls=%fused_computation.21 | convolution fusion | flops 336199680 | bytes 3932160 | tf_op jit(solution)/shard_map/hqk,khc->qhc/dot_general | solution.py:71
  104.6 2.2 %copy.45 = bf16[1,512,640]{2,1,0:T(8,128)(2,1)} copy(bf16[1,512,640]{1,2,0:T(8,128)(2,1)} %bitcast.84) | data formatting | bytes 1310720
  106.8 1.8 %convolution_convert_fusion.2 = bf16[5,128,512]{2,1,0:T(8,128)(2,1)} fusion(bf16[512,5,128]{0,2,1:T(8,128)(2,1)S(1)} %bitcast.79, bf16[5,512,512]{1,2,0:T(8,128)(2,1)S(1)} %fusion.10), kind=kOutput, calls=%fused_computation.24 | convolution fusion | flops 335872000 | bytes 3932160 | tf_op jit(solution)/shard_map/hqk,qhc->khc/dot_general | solution.py:62
  108.6 2.2 %copy.47 = bf16[1,512,640]{2,1,0:T(8,128)(2,1)} copy(bf16[1,512,640]{1,2,0:T(8,128)(2,1)} %bitcast.85) | data formatting | bytes 1310720
  110.7 6.0 %all-gather.4.cloned.1.call-done = bf16[5,128,1024]{2,1,0:T(8,128)(2,1)} async-done(((bf16[5,16,1024]{2,1,0:T(8,128)(2,1)}), bf16[5,128,1024]{2,1,0:T(8,128)(2,1)}) %all-gather.4.cloned.1.call-update) | async-done | bytes 1310736 | tf_op jit(solution)/shard_map/all_gather | solution.py:102
  116.7 2.5 %copy.67 = bf16[5,128,1024]{2,1,0:T(8,128)(2,1)} copy(bf16[5,128,1024]{2,1,0:T(8,128)(2,1)} %all-gather.4.cloned.1.call-done) | data formatting | bytes 2621440
  (12 shorter events, 0.0 us)
Async XLA Ops:
  7.2 3.7 %copy-start.3 = (bf16[1,512,640]{2,1,0:T(8,128)(2,1)S(1)}, bf16[1,512,640]{2,1,0:T(8,128)(2,1)}, u32[]{:S(2)}) copy-start(bf16[1,512,640]{2,1,0:T(8,128)(2,1)} %param.11) | copy-start | bytes 1966084
  7.2 33.1 %all-gather.6.cloned.1.call-start = ((), (), s32[]{:S(2)}) async-start(), calls=%async_computation.3 | async-start | bytes 1310720 | tf_op jit(solution)/shard_map/all_gather | solution.py:52
  7.9 82.2 %reduce-scatter.2.cloned.1.call-start = ((), (), s32[]{:S(2)}) async-start(), calls=%async_computation.1 | async-start | bytes 1474560 | tf_op jit(solution)/shard_map/reduce_scatter | solution.py:93
  9.3 6.8 %copy-start.4 = (bf16[1,512,640]{1,2,0:T(8,128)(2,1)}, bf16[1,512,640]{1,2,0:T(8,128)(2,1)S(1)}, u32[]{:S(2)}) copy-start(bf16[1,512,640]{1,2,0:T(8,128)(2,1)S(1)} %copy.32) | copy-start | bytes 1966084
  10.9 5.2 %copy-start.1 = (bf16[1,512,640]{1,2,0:T(8,128)(2,1)}, bf16[1,512,640]{1,2,0:T(8,128)(2,1)S(1)}, u32[]{:S(2)}) copy-start(bf16[1,512,640]{1,2,0:T(8,128)(2,1)S(1)} %copy.33) | copy-start | bytes 1966084
  45.1 1.8 %copy-start.2 = (bf16[5,128,1024]{2,1,0:T(8,128)(2,1)S(1)}, bf16[5,128,1024]{2,1,0:T(8,128)(2,1)}, u32[]{:S(2)}) copy-start(bf16[5,128,1024]{2,1,0:T(8,128)(2,1)} %param.16) | copy-start | bytes 3932164
  45.1 1.9 %copy-start.6 = (bf16[1,5,128,1024]{3,2,1,0:T(8,128)(2,1)S(1)}, bf16[1,5,128,1024]{3,2,1,0:T(8,128)(2,1)}, u32[]{:S(2)}) copy-start(bf16[1,5,128,1024]{3,2,1,0:T(8,128)(2,1)} %param.13) | copy-start | bytes 3932164
  45.1 2.3 %copy-start.7 = (bf16[1,5,128,1024]{3,2,1,0:T(8,128)(2,1)S(1)}, bf16[1,5,128,1024]{3,2,1,0:T(8,128)(2,1)}, u32[]{:S(2)}) copy-start(bf16[1,5,128,1024]{3,2,1,0:T(8,128)(2,1)} %param.14) | copy-start | bytes 3932164
  53.3 63.4 %all-gather.4.cloned.1.call-start = ((), (), s32[]{:S(2)}) async-start(), calls=%async_computation.2 | async-start | bytes 1474560 | tf_op jit(solution)/shard_map/all_gather | solution.py:102
  92.1 5.2 %copy-start.5 = (bf16[1,512,640]{1,2,0:T(8,128)(2,1)S(1)}, bf16[1,512,640]{1,2,0:T(8,128)(2,1)}, u32[]{:S(2)}) copy-start(bf16[1,512,640]{1,2,0:T(8,128)(2,1)} %copy-done.4) | copy-start | bytes 1966084
  95.8 1.5 %copy-start = (bf16[5,512,512]{1,2,0:T(8,128)(2,1)}, bf16[5,512,512]{1,2,0:T(8,128)(2,1)S(1)}, u32[]{:S(2)}) copy-start(bf16[5,512,512]{1,2,0:T(8,128)(2,1)S(1)} %multiply_convert_fusion) | copy-start | bytes 7864324
Sparse Core Ops, SparseCore 0:
  9.6 30.6 all-gather.5
  53.5 36.5 reduce-scatter.1
  92.2 24.4 all-gather.3
where the time goes:
time: 126 us
  waiting for transfers between devices  61.2 us (49%)
  matrix products  25.9 us (21%)
  local copies, waits for them, and re-layouts  16.4 us (13%)
  between operations  13.9 us (11%)
  other arithmetic  8.35 us (7%)
    reduce_scatter x1, waiting for transfers between devices, local(): lax.psum_scatter(delta_terms.astype(jnp.bfloat16), 'replica', scatter_dim...  33.6 us
    all_gather x1, waiting for transfers between devices, local(): block_rows = lax.all_gather(out_grads[0], 'tensor', axis=0, tiled=True)  20.9 us
    unnamed x23, local copies, waits for them, and re-layouts  15 us
    all_gather x1, waiting for transfers between devices, local(): new_anchor = lax.all_gather(updated, 'replica', axis=1, tiled=True)  5.99 us
    dot_general x1, matrix products, local(): lax.dot_general(attention_rows, block_rows, (((0,), (0,)), ((), ())), pre...  5.87 us
    sub x1, matrix products, local(): probs = jax.nn.softmax(scores, axis=-1)  4.12 us
    dot_general x1, matrix products, local(): jnp.einsum('qhc,khc->hqk', grad_attn, value_heads, preferred_element_type...  3.67 us
    dot_general x1, matrix products, local(): lax.dot_general(block_rows, proj_rows, (((1,), (1,)), ((), ())), preferre...  3.49 us
  transfers between devices with their start and end apart: 3, of which 3 were waited for; matrix products, arithmetic and copies ran while one was open for 25% of the time, Pallas kernels for 0%

commit v1 on v0

v1 whole, which is shorter than its diff:
```python
import functools
import math

import jax
import jax.numpy as jnp
from jax import lax
from jax.experimental import pallas as pl
from jax.experimental.pallas import tpu as pltpu
from jax.sharding import PartitionSpec as P

DH = 128
CHUNKS = 4
MESH = pl.DeviceIdType.MESH

beta_first = 0.9
beta_second = 0.95
correct_first = 0.9999734386011124
correct_second = 0.994079470779666
inner_rate = 0.01
decay_rate = 0.1
epsilon = 1e-08
outer_rate = 0.7
outer_beta = 0.9

F32 = jnp.float32
BF16 = jnp.bfloat16


def dot(a, b, ca, cb):
    return lax.dot_general(a, b, (((ca,), (cb,)), ((), ())), preferred_element_type=F32)


def kernel(
    tensors,
    workers,
    q_hbm, k_hbm, v_hbm, g_hbm, w_hbm, m1_hbm, m2_hbm, anchor_hbm, mom_hbm,
    dq_hbm, dk_hbm, dv_hbm, n1_hbm, n2_hbm, na_hbm, nm_hbm,
    q, k, v, g, w, m1, m2, anchor, mom,
    dq, dk, dv, n1, n2, na, nm,
    probs, att, att_t, ds, delta, from_partner, pair, from_peers,
    in_sem, out_sem,
    g_send, g_recv, p_send, p_recv, r_send, r_recv, a_send, a_recv, f_send, f_recv,
):
    heads = w.shape[0]
    width = g.shape[2]
    length = q.shape[0]
    rows = g.shape[1]
    slab = mom.shape[1]
    chips = workers // 2
    cw = width // CHUNKS
    scale = 1.0 / math.sqrt(DH)

    i = lax.axis_index("tensor")
    r = lax.axis_index("replica")
    chip = r // 2
    core = r % 2
    partner = chip * 2 + 1 - core
    has_left = i > 0
    has_right = i < tensors - 1

    def peer(step):
        return lax.rem(chip + step, chips) * 2 + core

    def source(step):
        return lax.rem(chip + chips - step, chips)

    barrier = pltpu.get_barrier_semaphore()

    @pl.when(has_left)
    def _():
        pl.semaphore_signal(barrier, inc=1, device_id={"tensor": i - 1}, device_id_type=MESH)

    @pl.when(has_right)
    def _():
        pl.semaphore_signal(barrier, inc=1, device_id={"tensor": i + 1}, device_id_type=MESH)

    pl.semaphore_signal(barrier, inc=1, device_id={"replica": partner}, device_id_type=MESH)
    for step in range(1, chips):
        pl.semaphore_signal(barrier, inc=1, device_id={"replica": peer(step)}, device_id_type=MESH)

    loads = [
        pltpu.make_async_copy(s, d, in_sem.at[n])
        for n, (s, d) in enumerate(
            [
                (q_hbm, q), (k_hbm, k), (v_hbm, v), (g_hbm, g.at[i]), (w_hbm, w),
                (m1_hbm, m1), (m2_hbm, m2), (anchor_hbm, anchor), (mom_hbm, mom),
            ]
        )
    ]
    for load in loads:
        load.start()

    inner = jnp.logical_and(has_left, has_right)

    @pl.when(inner)
    def _():
        pl.semaphore_wait(barrier, chips + 2)

    @pl.when(jnp.logical_not(inner))
    def _():
        pl.semaphore_wait(barrier, chips + 1)

    def cols(c):
        return pl.ds(c * cw, cw)

    def right_copy(block, s, c, own=False):
        src = g_hbm.at[:, cols(c)] if own else g.at[block, :, cols(c)]
        return pltpu.make_async_remote_copy(
            src_ref=src, dst_ref=g.at[block, :, cols(c)],
            send_sem=g_send.at[0, s, c], recv_sem=g_recv.at[0, s, c],
            device_id={"tensor": i + 1}, device_id_type=MESH,
        )

    def left_copy(block, s, c, own=False):
        src = g_hbm.at[:, cols(c)] if own else g.at[block, :, cols(c)]
        return pltpu.make_async_remote_copy(
            src_ref=src, dst_ref=g.at[block, :, cols(c)],
            send_sem=g_send.at[1, s, c], recv_sem=g_recv.at[1, s, c],
            device_id={"tensor": i - 1}, device_id_type=MESH,
        )

    def own_send(c):
        @pl.when(has_right)
        def _():
            right_copy(i, 0, c, True).start()

        @pl.when(has_left)
        def _():
            left_copy(i, 0, c, True).start()

    def relay(c, s):
        @pl.when(i - 1 - s >= 0)
        def _():
            block = i - 1 - s
            right_copy(block, s, c).wait_recv()
            if s + 1 <= tensors - 2:
                @pl.when(has_right)
                def _():
                    right_copy(block, s + 1, c).start()

        @pl.when(i + 1 + s < tensors)
        def _():
            block = i + 1 + s
            left_copy(block, s, c).wait_recv()
            if s + 1 <= tensors - 2:
                @pl.when(has_left)
                def _():
                    left_copy(block, s + 1, c).start()

    def drain_gather():
        for c in range(CHUNKS):
            for s in range(tensors - 1):
                @pl.when(jnp.logical_and(has_right, i - s >= 0))
                def _():
                    right_copy(i - s, s, c, s == 0).wait_send()

                @pl.when(jnp.logical_and(has_left, i + s < tensors))
                def _():
                    left_copy(i + s, s, c, s == 0).wait_send()

    tile = 128

    def forward(h):
        hc = pl.ds(h * DH, DH)
        kh = k[:, hc]
        vh = v[:, hc]
        for t in range(length // tile):
            tr = pl.ds(t * tile, tile)
            s = dot(q[tr, hc], kh, 1, 1) * scale
            e = jnp.exp(s - jnp.max(s, axis=-1, keepdims=True))
            p = (e / jnp.sum(e, axis=-1, keepdims=True)).astype(BF16)
            probs[h, tr, :] = p
            a = dot(p, vh, 1, 0)
            att[tr, hc] = a.astype(BF16)
            att_t[h, :, tr] = a.T.astype(BF16)

    def adam(c):
        def body(h, carry):
            gb = g[:, :, cols(c)].reshape(length, cw)
            grad = dot(att_t[h], gb, 1, 0)
            first = beta_first * m1[h, :, cols(c)].astype(F32) + (1.0 - beta_first) * grad
            second = (
                beta_second * m2[h, :, cols(c)].astype(F32) + (1.0 - beta_second) * grad * grad
            )
            n1[h, :, cols(c)] = first.astype(BF16)
            n2[h, :, cols(c)] = second.astype(BF16)
            old = w[h, :, cols(c)].astype(F32)
            stepped = old - inner_rate * (
                first / correct_first / (jnp.sqrt(second / correct_second) + epsilon)
                + decay_rate * old
            )
            an = anchor[h, :, :, cols(c)].astype(F32)
            d = an - stepped.reshape(workers, slab, cw)
            for x in range(workers):
                delta[c, x % 2, x // 2, h] = d[x].astype(BF16)
            return carry

        lax.fori_loop(0, heads, body, 0)

    def partner_copy(c):
        return pltpu.make_async_remote_copy(
            src_ref=delta.at[c, 1 - core], dst_ref=from_partner.at[c],
            send_sem=p_send.at[c], recv_sem=p_recv.at[c],
            device_id={"replica": partner}, device_id_type=MESH,
        )

    def peer_copy(c, step):
        return pltpu.make_async_remote_copy(
            src_ref=pair.at[c, lax.rem(chip + step, chips)], dst_ref=from_peers.at[c, step - 1],
            send_sem=r_send.at[c, step - 1], recv_sem=r_recv.at[c, step - 1],
            device_id={"replica": peer(step)}, device_id_type=MESH,
        )

    def pair_sum(c):
        partner_copy(c).wait_recv()
        for x in range(chips):
            pair[c, x] = (
                delta[c, core, x].astype(F32) + from_partner[c, x].astype(F32)
            ).astype(BF16)
        for step in range(1, chips):
            peer_copy(c, step).start()

    def spread(c, block, step):
        return pltpu.make_async_remote_copy(
            src_ref=na.at[:, block, :, cols(c)], dst_ref=na.at[:, block, :, cols(c)],
            send_sem=a_send.at[c, step - 1], recv_sem=a_recv.at[c, step - 1],
            device_id={"replica": peer(step)}, device_id_type=MESH,
        )

    def across(c, block, step):
        return pltpu.make_async_remote_copy(
            src_ref=na.at[:, block, :, cols(c)], dst_ref=na.at[:, block, :, cols(c)],
            send_sem=f_send.at[c, step], recv_sem=f_recv.at[c, step],
            device_id={"replica": partner}, device_id_type=MESH,
        )

    def outer(c):
        total = delta[c, core, chip].astype(F32) + from_partner[c, chip].astype(F32)
        for step in range(1, chips):
            peer_copy(c, step).wait_recv()
            total = total + from_peers[c, step - 1].astype(F32)
        average = total / workers
        moved = outer_beta * mom[:, :, cols(c)] + average
        nm[:, :, cols(c)] = moved
        part = anchor[:, r, :, cols(c)].astype(F32)
        na[:, r, :, cols(c)] = (
            part - outer_rate * (average + outer_beta * moved)
        ).astype(BF16)
        for step in range(1, chips):
            spread(c, r, step).start()
        across(c, r, 0).start()

    def pass_on(c):
        for step in range(1, chips):
            block = source(step) * 2 + core
            spread(c, block, step).wait_recv()
            across(c, block, step).start()

    def anchor_out(c):
        return pltpu.make_async_copy(
            na.at[:, :, :, cols(c)], na_hbm.at[:, :, :, cols(c)], out_sem.at[5 + c]
        )

    def finish(c):
        for step in range(chips):
            across(c, source(step) * 2 + 1 - core, step).wait_recv()
        anchor_out(c).start()

    def backward(h):
        hc = pl.ds(h * DH, DH)
        kh = k[:, hc]
        vh = v[:, hc]
        ga = dot(g[...].reshape(length, width), w[h], 1, 1).astype(BF16)
        for t in range(length // tile):
            tr = pl.ds(t * tile, tile)
            gt = ga[t * tile:(t + 1) * tile]
            row = jnp.sum(gt.astype(F32) * att[tr, hc].astype(F32), axis=-1, keepdims=True)
            gp = dot(gt, vh, 1, 1)
            s = (probs[h, tr, :].astype(F32) * (gp - row)).astype(BF16)
            ds[tr, :] = s
            dq[tr, hc] = (dot(s, kh, 1, 0) * scale).astype(BF16)
        dv[:, hc] = dot(ga, probs[h], 0, 0).T.astype(BF16)
        dk[:, hc] = (dot(q[:, hc], ds[...], 0, 0) * scale).T.astype(BF16)

    own_send(0)
    own_send(1)
    loads[0].wait()
    loads[1].wait()
    loads[2].wait()
    for h in range(heads):
        forward(h)
        if h < tensors - 1:
            relay(0, h)
    for s in range(heads, tensors - 1):
        relay(0, s)
    for load in loads[3:]:
        load.wait()
    for c in range(CHUNKS):
        if c > 0:
            for s in range(tensors - 1):
                relay(c, s)
        if c + 2 < CHUNKS:
            own_send(c + 2)
        adam(c)
        partner_copy(c).start()
        if c > 0:
            outer(c - 1)
        pair_sum(c)
        if c > 0:
            pass_on(c - 1)
    last = CHUNKS - 1
    stores = [
        pltpu.make_async_copy(s, d, out_sem.at[n])
        for n, (s, d) in enumerate([(dq, dq_hbm), (dk, dk_hbm), (dv, dv_hbm), (n1, n1_hbm), (n2, n2_hbm)])
    ]
    stores[3].start()
    stores[4].start()
    backward(0)
    backward(1)
    outer(last)
    backward(2)
    backward(3)
    pass_on(last)
    for h in range(4, heads):
        backward(h)
    store_mom = pltpu.make_async_copy(nm, nm_hbm, out_sem.at[5 + CHUNKS])
    store_mom.start()
    for store in stores[:3]:
        store.start()
    for c in range(CHUNKS):
        finish(c)
    drain_gather()
    for c in range(CHUNKS):
        partner_copy(c).wait_send()
        for step in range(1, chips):
            peer_copy(c, step).wait_send()
            spread(c, r, step).wait_send()
        for step in range(chips):
            across(c, source(step) * 2 + core, step).wait_send()
        anchor_out(c).wait()
    for store in stores:
        store.wait()
    store_mom.wait()


def local(tensors, workers, queries, key_rows, value_rows, out_grads, inner_weights, adam_first,
          adam_second, anchor, momentum):
    length, inner = queries.shape[1:]
    rows, width = out_grads.shape[1:]
    heads = inner_weights.shape[1]
    slab = momentum.shape[1]
    chips = workers // 2
    cw = width // CHUNKS
    qs = (length, inner)
    ws = (heads, DH, width)
    an = (heads, workers, slab, width)
    ms = (heads, slab, width)
    S = jax.ShapeDtypeStruct
    hbm = pl.BlockSpec(memory_space=pltpu.HBM)
    V = pltpu.VMEM
    D = pltpu.SemaphoreType.DMA
    outs = pl.pallas_call(
        functools.partial(kernel, tensors, workers),
        out_shape=[
            S(qs, BF16), S(qs, BF16), S(qs, BF16), S(ws, BF16), S(ws, BF16), S(an, BF16), S(ms, F32)
        ],
        in_specs=[hbm] * 9,
        out_specs=[hbm] * 7,
        scratch_shapes=[
            V(qs, BF16), V(qs, BF16), V(qs, BF16), V((tensors, rows, width), BF16),
            V(ws, BF16), V(ws, BF16), V(ws, BF16), V(an, BF16), V(ms, F32),
            V(qs, BF16), V(qs, BF16), V(qs, BF16), V(ws, BF16), V(ws, BF16), V(an, BF16), V(ms, F32),
            V((heads, length, length), BF16), V(qs, BF16), V((heads, DH, length), BF16),
            V((length, length), BF16),
            V((CHUNKS, 2, chips, heads, slab, cw), BF16),
            V((CHUNKS, chips, heads, slab, cw), BF16),
            V((CHUNKS, chips, heads, slab, cw), BF16),
            V((CHUNKS, chips - 1, heads, slab, cw), BF16),
            D((9,)), D((6 + CHUNKS,)),
            D((2, tensors - 1, CHUNKS)), D((2, tensors - 1, CHUNKS)),
            D((CHUNKS,)), D((CHUNKS,)),
            D((CHUNKS, chips - 1)), D((CHUNKS, chips - 1)),
            D((CHUNKS, chips - 1)), D((CHUNKS, chips - 1)),
            D((CHUNKS, chips)), D((CHUNKS, chips)),
        ],
        compiler_params=pltpu.CompilerParams(collective_id=0, has_side_effects=True),
        name="sync",
    )(
        queries[0], key_rows[0], value_rows[0], out_grads[0], inner_weights[0], adam_first[0],
        adam_second[0], anchor.reshape(an), momentum,
    )
    dq, dk, dv, n1, n2, na, nm = outs
    return dq[None], dk[None], dv[None], n1[None], n2[None], na.reshape(anchor.shape), nm


def solution(mesh):
    workers = P("replica", "tensor", None, None)
    heads = P("replica", None, "tensor")
    specs = (
        heads, heads, heads, P("replica", "tensor", None), workers, workers, workers,
        P("tensor", None, None), P("tensor", "replica", None),
    )
    outs = (
        heads, heads, heads, workers, workers, P("tensor", None, None), P("tensor", "replica", None)
    )
    body = functools.partial(local, mesh.shape["tensor"], mesh.shape["replica"])
    return jax.shard_map(body, mesh=mesh, in_specs=specs, out_specs=outs, check_vma=False)
```

time: 126 us -> 70.2 us (0.56)
  waiting for transfers between devices: 61.2 us -> 0 us
  Pallas kernels: 0 us -> 60.1 us
  matrix products: 25.9 us -> 0 us
  between operations: 13.9 us -> 0.67 us
  other arithmetic: 8.35 us -> 0 us
  local copies, waits for them, and re-layouts: 16.4 us -> 9.23 us
    pallas_call x0 -> x1, Pallas kernels: none -> 60.1 us  [local(): pl.pallas_call(functools.partial(kernel, tensors, workers), out_shape=[S(...]
    reduce_scatter x1 -> x0, waiting for transfers between devices: 33.6 us -> none  [local(): lax.psum_scatter(delta_terms.astype(jnp.bfloat16), 'replica', scatter_dim...]
    all_gather x2 -> x0, waiting for transfers between devices: 26.9 us -> none  [the longest x1 20.9 us: local(): block_rows = lax.all_gather(out_grads[0], 'tensor', axis=0, tiled=True)]
    dot_general x7 -> x0, matrix products: 21.7 us -> none  [the longest x1 5.87 us: local(): lax.dot_general(attention_rows, block_rows, (((0,), (0,)), ((), ())), pre...]
    convert_element_type x3 -> x0, other arithmetic: 8.35 us -> none  [the longest x1 3.22 us: local(): probs_low = probs.astype(jnp.bfloat16)]
    unnamed x23 -> x19, local copies, waits for them, and re-layouts: 15 us -> 9.23 us
    sub x1 -> x0, matrix products: 4.12 us -> none  [local(): probs = jax.nn.softmax(scores, axis=-1)]
    convert_element_type x1 -> x0, local copies, waits for them, and re-layouts: 1.33 us -> none  [local(): product_rows = lax.dot_general(block_rows, proj_rows, (((1,), (1,)), ((),...]
  transfers between devices with their start and end apart: 3 -> 0, of which waited for: 3 -> 0; matrix products, arithmetic and copies ran while one was open for 25% -> 0% of each run, Pallas kernels for 0% -> 0%
where the time goes in v1:
time: 70.2 us; the launch traced here: 70 us
  Pallas kernels  60.1 us (86%)
  local copies, waits for them, and re-layouts  9.23 us (13%)
    pallas_call x1, Pallas kernels, local(): pl.pallas_call(functools.partial(kernel, tensors, workers), out_shape=[S(...  60.1 us
    unnamed x19, local copies, waits for them, and re-layouts  9.23 us

profile of v1, /device:TPU:0, one launch (start us, length us, event | category | flops | bytes accessed | tf_op | source)
XLA Modules:
  0.0 70.0 jit_solution(9016770591850387892)
XLA Ops:
  0.6 60.1 %sync.1 = (bf16[512,640]{1,0:T(8,128)(2,1)}, bf16[512,640]{1,0:T(8,128)(2,1)}, bf16[512,640]{1,0:T(8,128)(2,1)}, bf16[5,128,1024]{2,1,0:T(8,128)(2,1)}, bf16[5,1...) custom-call(bf16[512,640]{1,0:T(8,128)(2,1)} %bitcast.24, ...), custom_call_target="tpu_custom_call" | custom-call | tf_op jit(solution)/shard_map/sync/pallas_call | solution.py:362
  60.7 0.0 copy-start.4
  60.7 0.0 copy-start.3
  60.7 2.1 %copy.23 = bf16[1,512,640]{2,1,0:T(8,128)(2,1)} copy(bf16[1,512,640]{2,1,0:T(8,128)(2,1)} %bitcast.23) | data formatting | bytes 1310720
  62.8 0.0 copy-done.4
  62.8 0.0 copy-start.2
  62.8 0.8 %copy.24 = bf16[1,512,640]{2,1,0:T(8,128)(2,1)} copy(bf16[1,512,640]{2,1,0:T(8,128)(2,1)S(1)} %bitcast.22) | data formatting | bytes 1310720
  63.6 0.0 copy-done.3
  63.6 0.8 %copy.25 = bf16[1,512,640]{2,1,0:T(8,128)(2,1)} copy(bf16[1,512,640]{2,1,0:T(8,128)(2,1)S(1)} %bitcast.21) | data formatting | bytes 1310720
  64.5 0.0 copy-done.2
  64.5 0.0 copy-start.1
  64.5 1.1 %copy.26 = bf16[1,5,128,1024]{3,2,1,0:T(8,128)(2,1)} copy(bf16[1,5,128,1024]{3,2,1,0:T(8,128)(2,1)S(1)} %bitcast.16) | data formatting | bytes 2621440
  65.5 0.7 %copy-done.1 = bf16[5,128,1024]{2,1,0:T(8,128)(2,1)S(1)} copy-done((bf16[5,128,1024]{2,1,0:T(8,128)(2,1)S(1)}, bf16[5,128,1024]{2,1,0:T(8,128)(2,1)}, u32[]{:S(2)}) %copy-start.1) | copy-done | bytes 1310744
  66.3 0.0 copy-start
  66.3 1.1 %copy.27 = bf16[1,5,128,1024]{3,2,1,0:T(8,128)(2,1)} copy(bf16[1,5,128,1024]{3,2,1,0:T(8,128)(2,1)S(1)} %bitcast.15) | data formatting | bytes 2621440
  67.3 0.7 %copy-done = bf16[5,8,16,1024]{3,2,1,0:T(8,128)(2,1)S(1)} copy-done((bf16[5,8,16,1024]{3,2,1,0:T(8,128)(2,1)S(1)}, bf16[5,8,16,1024]{3,2,1,0:T(8,128)(2,1)}, u32[]{:S(2)}) %copy-start) | copy-done | bytes 1310744
  68.1 0.0 copy-start.5
  68.1 1.1 %copy.28 = bf16[5,128,1024]{2,1,0:T(8,128)(2,1)} copy(bf16[5,128,1024]{2,1,0:T(8,128)(2,1)S(1)} %bitcast.14) | data formatting | bytes 2621440
  69.1 0.1 copy-done.5
  69.2 0.7 %copy.29 = f32[5,16,1024]{2,1,0:T(8,128)} copy(f32[5,16,1024]{2,1,0:T(8,128)S(1)} %copy-done.5) | data formatting | bytes 655360
Async XLA Ops:
  60.7 2.1 %copy-start.4 = (bf16[512,640]{1,0:T(8,128)(2,1)S(1)}, bf16[512,640]{1,0:T(8,128)(2,1)}, u32[]{:S(2)}) copy-start(bf16[512,640]{1,0:T(8,128)(2,1)} %get-tuple-element.15) | copy-start | bytes 1966084
  60.7 2.9 %copy-start.3 = (bf16[512,640]{1,0:T(8,128)(2,1)S(1)}, bf16[512,640]{1,0:T(8,128)(2,1)}, u32[]{:S(2)}) copy-start(bf16[512,640]{1,0:T(8,128)(2,1)} %get-tuple-element.16) | copy-start | bytes 1966084
  62.8 1.7 %copy-start.2 = (bf16[5,128,1024]{2,1,0:T(8,128)(2,1)S(1)}, bf16[5,128,1024]{2,1,0:T(8,128)(2,1)}, u32[]{:S(2)}) copy-start(bf16[5,128,1024]{2,1,0:T(8,128)(2,1)} %get-tuple-element.17) | copy-start | bytes 3932164
  64.5 1.8 %copy-start.1 = (bf16[5,128,1024]{2,1,0:T(8,128)(2,1)S(1)}, bf16[5,128,1024]{2,1,0:T(8,128)(2,1)}, u32[]{:S(2)}) copy-start(bf16[5,128,1024]{2,1,0:T(8,128)(2,1)} %get-tuple-element.18) | copy-start | bytes 3932164
  66.3 1.8 %copy-start = (bf16[5,8,16,1024]{3,2,1,0:T(8,128)(2,1)S(1)}, bf16[5,8,16,1024]{3,2,1,0:T(8,128)(2,1)}, u32[]{:S(2)}) copy-start(bf16[5,8,16,1024]{3,2,1,0:T(8,128)(2,1)} %get-tuple-element.19) | copy-start | bytes 3932164
  68.1 1.2 %copy-start.5 = (f32[5,16,1024]{2,1,0:T(8,128)S(1)}, f32[5,16,1024]{2,1,0:T(8,128)}, u32[]{:S(2)}) copy-start(f32[5,16,1024]{2,1,0:T(8,128)} %get-tuple-element.34) | copy-start | bytes 983044

commit v2 on v1

--- a/solution.py
+++ b/solution.py
@@ -9,7 +9,10 @@
 from jax.sharding import PartitionSpec as P
 
 DH = 128
-CHUNKS = 4
+CHUNKS = 2
+TILE = 512
+VMEM_BYTES = 67043328
+SPARE = 2**17
 MESH = pl.DeviceIdType.MESH
 
 beta_first = 0.9
@@ -34,11 +37,10 @@
     tensors,
     workers,
     q_hbm, k_hbm, v_hbm, g_hbm, w_hbm, m1_hbm, m2_hbm, anchor_hbm, mom_hbm,
-    dq_hbm, dk_hbm, dv_hbm, n1_hbm, n2_hbm, na_hbm, nm_hbm,
+    dq, dk, dv, n1, n2, na, nm,
     q, k, v, g, w, m1, m2, anchor, mom,
-    dq, dk, dv, n1, n2, na, nm,
     probs, att, att_t, ds, delta, from_partner, pair, from_peers,
-    in_sem, out_sem,
+    in_sem,
     g_send, g_recv, p_send, p_recv, r_send, r_recv, a_send, a_recv, f_send, f_recv,
 ):
     heads = w.shape[0]
@@ -158,7 +160,7 @@
                 def _():
                     left_copy(i + s, s, c, s == 0).wait_send()
 
-    tile = 128
+    tile = TILE
 
     def forward(h):
         hc = pl.ds(h * DH, DH)
@@ -256,15 +258,9 @@
             spread(c, block, step).wait_recv()
             across(c, block, step).start()
 
-    def anchor_out(c):
-        return pltpu.make_async_copy(
-            na.at[:, :, :, cols(c)], na_hbm.at[:, :, :, cols(c)], out_sem.at[5 + c]
-        )
-
     def finish(c):
         for step in range(chips):
             across(c, source(step) * 2 + 1 - core, step).wait_recv()
-        anchor_out(c).start()
 
     def backward(h):
         hc = pl.ds(h * DH, DH)
@@ -282,11 +278,11 @@
         dv[:, hc] = dot(ga, probs[h], 0, 0).T.astype(BF16)
         dk[:, hc] = (dot(q[:, hc], ds[...], 0, 0) * scale).T.astype(BF16)
 
-    own_send(0)
-    own_send(1)
-    loads[0].wait()
-    loads[1].wait()
-    loads[2].wait()
+    ahead = min(2, CHUNKS)
+    for c in range(ahead):
+        own_send(c)
+    for load in loads[:3]:
+        load.wait()
     for h in range(heads):
         forward(h)
         if h < tensors - 1:
@@ -295,38 +291,30 @@
         relay(0, s)
     for load in loads[3:]:
         load.wait()
+    stages = (pass_on, outer, pair_sum)
+
+    def sync(slot, which):
+        c = slot - (3 - which)
+        if 0 <= c < CHUNKS:
+            stages[which](c)
+
     for c in range(CHUNKS):
         if c > 0:
             for s in range(tensors - 1):
                 relay(c, s)
-        if c + 2 < CHUNKS:
-            own_send(c + 2)
+        if c + ahead < CHUNKS:
+            own_send(c + ahead)
+        for which in range(3):
+            sync(c, which)
         adam(c)
         partner_copy(c).start()
-        if c > 0:
-            outer(c - 1)
-        pair_sum(c)
-        if c > 0:
-            pass_on(c - 1)
-    last = CHUNKS - 1
-    stores = [
-        pltpu.make_async_copy(s, d, out_sem.at[n])
-        for n, (s, d) in enumerate([(dq, dq_hbm), (dk, dk_hbm), (dv, dv_hbm), (n1, n1_hbm), (n2, n2_hbm)])
-    ]
-    stores[3].start()
-    stores[4].start()
-    backward(0)
-    backward(1)
-    outer(last)
-    backward(2)
-    backward(3)
-    pass_on(last)
-    for h in range(4, heads):
+    for h in range(heads):
         backward(h)
-    store_mom = pltpu.make_async_copy(nm, nm_hbm, out_sem.at[5 + CHUNKS])
-    store_mom.start()
-    for store in stores[:3]:
-        store.start()
+        for which in range(3):
+            sync(CHUNKS + h, which)
+    for slot in range(CHUNKS + heads, CHUNKS + 3):
+        for which in range(3):
+            sync(slot, which)
     for c in range(CHUNKS):
         finish(c)
     drain_gather()
@@ -337,10 +325,14 @@
             spread(c, r, step).wait_send()
         for step in range(chips):
             across(c, source(step) * 2 + core, step).wait_send()
-        anchor_out(c).wait()
-    for store in stores:
-        store.wait()
-    store_mom.wait()
+
+def store(*refs):
+    n = (len(refs) - 1) // 2
+    copies = [pltpu.make_async_copy(refs[j], refs[n + j], refs[-1].at[j]) for j in range(n)]
+    for copy in copies:
+        copy.start()
+    for copy in copies:
+        copy.wait()
 
 
 def local(tensors, workers, queries, key_rows, value_rows, out_grads, inner_weights, adam_first,
@@ -359,37 +351,45 @@
     hbm = pl.BlockSpec(memory_space=pltpu.HBM)
     V = pltpu.VMEM
     D = pltpu.SemaphoreType.DMA
+    results = [(qs, BF16)] * 3 + [(ws, BF16)] * 2 + [(an, BF16), (ms, F32)]
+    held = sum(math.prod(shape) * jnp.dtype(dtype).itemsize for shape, dtype in results)
+    room = VMEM_BYTES - held - SPARE
     outs = pl.pallas_call(
         functools.partial(kernel, tensors, workers),
-        out_shape=[
-            S(qs, BF16), S(qs, BF16), S(qs, BF16), S(ws, BF16), S(ws, BF16), S(an, BF16), S(ms, F32)
-        ],
+        out_shape=[V(shape, dtype) for shape, dtype in results],
         in_specs=[hbm] * 9,
-        out_specs=[hbm] * 7,
+        out_specs=[pl.BlockSpec(memory_space=V)] * 7,
         scratch_shapes=[
             V(qs, BF16), V(qs, BF16), V(qs, BF16), V((tensors, rows, width), BF16),
             V(ws, BF16), V(ws, BF16), V(ws, BF16), V(an, BF16), V(ms, F32),
-            V(qs, BF16), V(qs, BF16), V(qs, BF16), V(ws, BF16), V(ws, BF16), V(an, BF16), V(ms, F32),
             V((heads, length, length), BF16), V(qs, BF16), V((heads, DH, length), BF16),
             V((length, length), BF16),
             V((CHUNKS, 2, chips, heads, slab, cw), BF16),
             V((CHUNKS, chips, heads, slab, cw), BF16),
             V((CHUNKS, chips, heads, slab, cw), BF16),
             V((CHUNKS, chips - 1, heads, slab, cw), BF16),
-            D((9,)), D((6 + CHUNKS,)),
+            D((9,)),
             D((2, tensors - 1, CHUNKS)), D((2, tensors - 1, CHUNKS)),
             D((CHUNKS,)), D((CHUNKS,)),
             D((CHUNKS, chips - 1)), D((CHUNKS, chips - 1)),
             D((CHUNKS, chips - 1)), D((CHUNKS, chips - 1)),
             D((CHUNKS, chips)), D((CHUNKS, chips)),
         ],
-        compiler_params=pltpu.CompilerParams(collective_id=0, has_side_effects=True),
+        compiler_params=pltpu.CompilerParams(collective_id=0, has_side_effects=True, vmem_limit_bytes=room),
         name="sync",
     )(
         queries[0], key_rows[0], value_rows[0], out_grads[0], inner_weights[0], adam_first[0],
         adam_second[0], anchor.reshape(an), momentum,
     )
-    dq, dk, dv, n1, n2, na, nm = outs
+    dq, dk, dv, n1, n2, na, nm = pl.pallas_call(
+        store,
+        out_shape=[S(shape, dtype) for shape, dtype in results],
+        in_specs=[pl.BlockSpec(memory_space=V)] * 7,
+        out_specs=[hbm] * 7,
+        scratch_shapes=[D((7,))],
+        compiler_params=pltpu.CompilerParams(vmem_limit_bytes=2**20),
+        name="store",
+    )(*outs)
     return dq[None], dk[None], dv[None], n1[None], n2[None], na.reshape(anchor.shape), nm
 
 

time: 70.2 us -> 51.4 us (0.73)
  Pallas kernels: 60.1 us -> 50.6 us
  local copies, waits for them, and re-layouts: 9.23 us -> 0 us
    pallas_call x1 -> x2, Pallas kernels: 60.1 us -> 50.6 us  [the longest x1 47.9 us: local(): pl.pallas_call(functools.partial(kernel, tensors, workers), out_shape=[V(...]
    unnamed x19 -> x0, local copies, waits for them, and re-layouts: 9.23 us -> none
where the time goes in v2:
time: 51.4 us; the launch traced here: 51.3 us
  Pallas kernels  50.6 us (98%)
  between operations  0.64 us (1%)
    pallas_call x1, Pallas kernels, local(): pl.pallas_call(functools.partial(kernel, tensors, workers), out_shape=[V(...  47.9 us
    pallas_call x1, Pallas kernels, local(): pl.pallas_call(store, out_shape=[S(shape, dtype) for shape, dtype in resu...  2.69 us

profile of v2, /device:TPU:0, one launch (start us, length us, event | category | flops | bytes accessed | tf_op | source)
XLA Modules:
  0.0 51.3 jit_solution(3469542600771973248)
XLA Ops:
  0.6 47.9 %sync.1 = (bf16[512,640]{1,0:T(8,128)(2,1)S(1)}, bf16[512,640]{1,0:T(8,128)(2,1)S(1)}, bf16[512,640]{1,0:T(8,128)(2,1)S(1)}, bf16[5,128,1024]{2,1,0:T(8,128)(2,1...) custom-call(bf16[512,640]{1,0:T(8,128)(2,1)} %bitcast.18, ...), custom_call_target="tpu_custom_call" | custom-call | tf_op jit(solution)/shard_map/sync/pallas_call | solution.py:357
  48.6 2.7 %store.1 = (bf16[512,640]{1,0:T(8,128)(2,1)}, bf16[512,640]{1,0:T(8,128)(2,1)}, bf16[512,640]{1,0:T(8,128)(2,1)}, bf16[5,128,1024]{2,1,0:T(8,128)(2,1)}, bf16[5,...) custom-call(bf16[512,640]{1,0:T(8,128)(2,1)S(1)} %get-tuple-element.21.refs_0_, ...), custom_call_target="tpu_custom_call" | custom-call | tf_op jit(solution)/shard_map/store/pallas_call | solution.py:384

commit v3 on v2

--- a/solution.py
+++ b/solution.py
@@ -291,30 +291,31 @@
         relay(0, s)
     for load in loads[3:]:
         load.wait()
-    stages = (pass_on, outer, pair_sum)
-
-    def sync(slot, which):
-        c = slot - (3 - which)
-        if 0 <= c < CHUNKS:
-            stages[which](c)
-
     for c in range(CHUNKS):
         if c > 0:
             for s in range(tensors - 1):
+                if s == tensors - 2:
+                    pair_sum(c - 1)
                 relay(c, s)
         if c + ahead < CHUNKS:
             own_send(c + ahead)
-        for which in range(3):
-            sync(c, which)
         adam(c)
         partner_copy(c).start()
+        if c > 0:
+            outer(c - 1)
+        if 0 < c < CHUNKS - 1:
+            pass_on(c - 1)
+    last = CHUNKS - 1
     for h in range(heads):
         backward(h)
-        for which in range(3):
-            sync(CHUNKS + h, which)
-    for slot in range(CHUNKS + heads, CHUNKS + 3):
-        for which in range(3):
-            sync(slot, which)
+        if h == 0:
+            pair_sum(last)
+        if h == min(1, heads - 1):
+            if CHUNKS > 1:
+                pass_on(last - 1)
+            outer(last)
+        if h == min(3, heads - 1):
+            pass_on(last)
     for c in range(CHUNKS):
         finish(c)
     drain_gather()

time: 51.4 us -> 49.8 us (0.969)
  Pallas kernels: 50.6 us -> 49 us
    pallas_call x1, Pallas kernels: 47.9 us -> 46.3 us  [local(): pl.pallas_call(functools.partial(kernel, tensors, workers), out_shape=[V(...]
where the time goes in v3:
time: 49.8 us; the launch traced here: 49.7 us
  Pallas kernels  49 us (98%)
  between operations  0.64 us (1%)
    pallas_call x1, Pallas kernels, local(): pl.pallas_call(functools.partial(kernel, tensors, workers), out_shape=[V(...  46.3 us
    pallas_call x1, Pallas kernels, local(): pl.pallas_call(store, out_shape=[S(shape, dtype) for shape, dtype in resu...  2.69 us

profile of v3, /device:TPU:0, one launch (start us, length us, event | category | flops | bytes accessed | tf_op | source)
XLA Modules:
  0.0 49.7 jit_solution(12479068054830374497)
XLA Ops:
  0.6 46.3 %sync.1 = (bf16[512,640]{1,0:T(8,128)(2,1)S(1)}, bf16[512,640]{1,0:T(8,128)(2,1)S(1)}, bf16[512,640]{1,0:T(8,128)(2,1)S(1)}, bf16[5,128,1024]{2,1,0:T(8,128)(2,1...) custom-call(bf16[512,640]{1,0:T(8,128)(2,1)} %bitcast.18, ...), custom_call_target="tpu_custom_call" | custom-call | tf_op jit(solution)/shard_map/sync/pallas_call | solution.py:358
  47.0 2.7 %store.1 = (bf16[512,640]{1,0:T(8,128)(2,1)}, bf16[512,640]{1,0:T(8,128)(2,1)}, bf16[512,640]{1,0:T(8,128)(2,1)}, bf16[5,128,1024]{2,1,0:T(8,128)(2,1)}, bf16[5,...) custom-call(bf16[512,640]{1,0:T(8,128)(2,1)S(1)} %get-tuple-element.21.refs_0_, ...), custom_call_target="tpu_custom_call" | custom-call | tf_op jit(solution)/shard_map/store/pallas_call | solution.py:385
